TPU v7x, 512 devices: a whole 4x4x16 slice. The times are simulated.
512 devices in a mesh: req: 64 (over z, y), tensor: 8 (over x, core).
Axes of the slice: x: 4, y: 4, z: 16, core: 2. Of those that a mesh axis runs over, the one named last changes fastest.
Arguments:
- tokens: bfloat16 [16384, 2048], P('req', 'tensor'), may hold values from -6 to 6
- segment_ids: int32 [16384], P('req'), may hold values from 0 to 42, as said below
- prefix_lengths: int32 [43], replicated, may hold values from 0 to 256, as said below
- page_owner: int32 [4096, 1], P('req'), may hold values from 0 to 63; in each aligned block of 64 rows (0 to 63, 64 to 127, ...) at most 2 rows name the same one
- slot_perm: int32 [64, 128], P('req'), may hold values from 0 to 127, each once within a row
- ln_gain: float32 [2048], replicated, may hold values from 0.1 to 1.9
- ln_bias: float32 [2048], replicated, may hold values from -3 to 3
- qkv_weight: bfloat16 [2048, 3, 2048], P('req', None, 'tensor')
- qkv_bias: float32 [3, 2048], P(None, 'tensor'), may hold values from -3 to 3
- dense_weight: bfloat16 [2048, 2048], P('tensor', 'req'), may hold values from -0.375 to 0.375
- dense_bias: float32 [2048], P('tensor'), may hold values from -3 to 3
- fc1_weight: bfloat16 [2048, 4096], P('req', 'tensor'), may hold values from -0.125 to 0.125
- fc1_bias: float32 [4096], P('tensor'), may hold values from -3 to 3
- fc2_weight: bfloat16 [4096, 2048], P('tensor', 'req'), may hold values from -0.25 to 0.25
- fc2_bias: float32 [2048], P('tensor'), may hold values from -3 to 3
- prefix_cache: bfloat16 [16384, 2, 2048], P('req', None, 'tensor'), may hold values from -9 to 9
- cache_pool: bfloat16 [32768, 2, 2048], P('req', None, 'tensor'), may hold values from -6 to 6
Outputs:
- layer_out: bfloat16 [16384, 2048], P('req', 'tensor')
- new_pool: bfloat16 [32768, 2, 2048], P('req', None, 'tensor')
Inputs may be any that keep to these rules, and one draw needn't show every extreme that they name: `segment_ids`: labels 1 to 42 appear in order, each as one run of 257 to 512 rows, together filling all rows before the padding; segment 1 is 512 rows long; the last 128 rows are 0. `prefix_lengths`: entry 0 is 0 and entry 1 is 256. `page_owner`: among the pages of one index of req no owner appears more than 2 times, and some owner appears exactly 2 times. `slot_perm`: each row is a permutation of 0 to 127.
All inputs are finite; a program needn't handle non-finite values.
Results may differ from a plain program's by a relative error of at most 0.006.
The roundings to bfloat16 on the way count: a program that leaves them out, or rounds other values in their place, can miss the bound.
Values may be sent and summed in bfloat16 or wider, within the bound.
A program may use at most 64 MiB of HBM per device.

v0:
```python
import jax
import jax.numpy as jnp
from jax import lax
from jax.sharding import PartitionSpec as P

HEAD_DIM = 64
ROT = 32
SPAN = 2
SINKS = 4
PAGE = 4
WINDOW = 512
EPSILON = 1e-05


def from_behind(value, axis, steps):
    count = lax.axis_size(axis)
    leading, last = (max(0, -steps), min(count, count - steps))
    return lax.ppermute(value, axis, [(source, source + steps) for source in range(leading, last)])


def norm_rows(widened, gain, offset_bias):
    average = jnp.mean(widened, axis=-1, keepdims=True)
    centred = widened - average
    spread = jnp.mean(centred * centred, axis=-1, keepdims=True)
    return (centred * lax.rsqrt(spread + EPSILON) * gain + offset_bias).astype(jnp.bfloat16)


def label_rows(places, starts, prefix_lengths):
    labels = jnp.arange(starts.shape[0], dtype=jnp.int32)
    passed = (starts[None, :] <= places[:, None]) & (labels[None, :] >= 1)
    counted = jnp.sum(passed.astype(jnp.int32), axis=1)
    segment = jnp.where(places >= starts[0], 0, counted)
    segment = jnp.where(places < 0, -2, segment)
    onehot = segment[:, None] == labels[None, :]
    earliest = jnp.sum(jnp.where(onehot, starts[None, :], 0), axis=1)
    offset = jnp.sum(jnp.where(onehot, prefix_lengths[None, :], 0), axis=1)
    return (segment, offset + places - earliest)


def prefix_rows(block_id, rows_dev, prefix_count, starts, prefix_lengths):
    labels = jnp.arange(starts.shape[0], dtype=jnp.int32)
    located = (starts >= block_id * rows_dev) & (starts < (block_id + 1) * rows_dev) & (labels >= 1)
    owner_label = jnp.sum(jnp.where(located, labels, 0))
    length = jnp.sum(jnp.where(located, prefix_lengths, 0))
    places = jnp.arange(prefix_count, dtype=jnp.int32)
    usable = jnp.any(located) & (places < length)
    return (jnp.where(usable, owner_label, -2), places)


def rotate_heads(values, position):
    half_rot = ROT // 2
    frequency = 10000.0 ** (-2.0 * jnp.arange(half_rot, dtype=jnp.float32) / ROT)
    angles = position.astype(jnp.float32)[:, None] * frequency[None, :]
    cosine = jnp.cos(angles)[:, None, :]
    sine_vals = jnp.sin(angles)[:, None, :]
    lower = values[..., :half_rot]
    upper = values[..., half_rot:ROT]
    return jnp.concatenate(
        [lower * cosine - upper * sine_vals, upper * cosine + lower * sine_vals, values[..., ROT:]],
        axis=-1,
    )


def head_attention(query_rows, key_rows, value_rows, allowed):
    head_count = query_rows.shape[1] // HEAD_DIM
    score_scale = HEAD_DIM ** (-0.5)

    def one_head(head_index):
        query_cols = lax.dynamic_slice_in_dim(query_rows, head_index * HEAD_DIM, HEAD_DIM, 1)
        key_cols = lax.dynamic_slice_in_dim(key_rows, head_index * HEAD_DIM, HEAD_DIM, 1)
        value_cols = lax.dynamic_slice_in_dim(value_rows, head_index * HEAD_DIM, HEAD_DIM, 1)
        scores = (
            lax.dot_general(
                query_cols, key_cols, (((1,), (1,)), ((), ())), preferred_element_type=jnp.float32
            )
            * score_scale
        )
        masked = jnp.where(allowed, scores, -1e30)
        highest = jnp.max(masked, axis=1, keepdims=True)
        expo = jnp.where(allowed, jnp.exp(masked - highest), 0.0)
        denom = jnp.sum(expo, axis=1, keepdims=True)
        mixed = (
            jnp.dot(expo.astype(jnp.bfloat16), value_cols, preferred_element_type=jnp.float32)
            / denom
        )
        return mixed.astype(jnp.bfloat16)

    outcome = lax.map(one_head, jnp.arange(head_count, dtype=jnp.int32))
    return jnp.transpose(outcome, (1, 0, 2)).reshape(query_rows.shape[0], head_count * HEAD_DIM)


def shards(
    tokens,
    segment_ids,
    prefix_lengths,
    page_owner,
    slot_perm,
    ln_gain,
    ln_bias,
    qkv_weight,
    qkv_bias,
    dense_weight,
    dense_bias,
    fc1_weight,
    fc1_bias,
    fc2_weight,
    fc2_bias,
    prefix_cache,
    cache_pool,
):
    req_count = lax.axis_size("req")
    req_index = lax.axis_index("req")
    tok_rows = tokens.shape[0]
    prefix_count = prefix_cache.shape[0]
    head_cols = qkv_weight.shape[2]
    pool_count = slot_perm.shape[1]
    page_cap = pool_count // req_count
    gathered = lax.all_gather(tokens, "tensor", axis=1, tiled=True)
    normed = norm_rows(gathered.astype(jnp.float32), ln_gain, ln_bias)
    row_ids = jnp.arange(tok_rows, dtype=jnp.int32)
    places = req_index * tok_rows + row_ids
    labels = jnp.arange(prefix_lengths.shape[0], dtype=jnp.int32)
    label_count = labels.shape[0]
    beyond = tok_rows * req_count
    earliest_rows = jnp.min(
        jnp.where(segment_ids[:, None] == labels[None, :], places[:, None], beyond), axis=0
    )
    weight_rows = qkv_weight.shape[0]
    digit_cols = 128
    digits = jnp.concatenate([earliest_rows // 128, earliest_rows % 128]).astype(jnp.bfloat16)
    digits = jnp.pad(digits, (0, weight_rows * digit_cols - 2 * label_count)).reshape(
        weight_rows, digit_cols
    )
    qkv_local = qkv_weight.reshape(weight_rows, 3 * head_cols)
    fc1_cols = fc1_weight.shape[1]
    dense_cols = dense_weight.shape[0]
    fc2_cols = fc2_weight.shape[0]
    packed = jnp.concatenate([qkv_local, fc1_weight, dense_weight.T, fc2_weight.T, digits], axis=1)
    everything = lax.all_gather(packed, "req", axis=0, tiled=True)
    edges = [0]
    for width in (3 * head_cols, fc1_cols, dense_cols, fc2_cols, digit_cols):
        edges.append(edges[-1] + width)
    qkv_full, fc1_full, dense_full_t, fc2_full_t, digits_full = [
        everything[:, edges[i] : edges[i + 1]] for i in range(5)
    ]
    digit_table = digits_full.reshape(req_count, weight_rows * digit_cols)[:, : 2 * label_count]
    digit_table = digit_table.astype(jnp.int32)
    starts = jnp.min(digit_table[:, :label_count] * 128 + digit_table[:, label_count:], axis=0)

    def add_rows(portion):
        return jnp.dot(normed, portion, preferred_element_type=jnp.float32)

    projected = add_rows(qkv_full)
    lifted = add_rows(fc1_full)
    projected = (projected + qkv_bias.reshape(1, 3 * head_cols)).reshape(
        tok_rows, 3, head_cols // HEAD_DIM, HEAD_DIM
    )
    segment, position = label_rows(places, starts, prefix_lengths)
    queries = (
        rotate_heads(projected[:, 0], position).astype(jnp.bfloat16).reshape(tok_rows, head_cols)
    )
    new_keys = (
        rotate_heads(projected[:, 1], position).astype(jnp.bfloat16).reshape(tok_rows, head_cols)
    )
    new_values = projected[:, 2].astype(jnp.bfloat16).reshape(tok_rows, head_cols)
    key_value = jnp.stack([new_keys, new_values], axis=1)
    pages_here = tok_rows // PAGE
    page_width = PAGE * 2 * head_cols
    pages = key_value.reshape(pages_here, page_width)
    owners = page_owner[:, 0]
    onehot = (owners[:, None] == jnp.arange(req_count, dtype=jnp.int32)[None, :]).astype(jnp.int32)
    earlier = jnp.cumsum(onehot, axis=0) - onehot
    earlier_count = jnp.sum(earlier * onehot, axis=1)
    target = owners * page_cap + earlier_count
    selecting = (target[None, :] == jnp.arange(pool_count, dtype=jnp.int32)[:, None]).astype(
        jnp.bfloat16
    )
    outgoing = jnp.dot(selecting, pages, preferred_element_type=jnp.float32).astype(jnp.bfloat16)
    filled = jnp.sum(selecting, axis=1)
    flag_cols = 128
    flagged = jnp.concatenate(
        [outgoing, jnp.broadcast_to(filled[:, None], (pool_count, flag_cols)).astype(jnp.bfloat16)],
        axis=1,
    )
    arrived = lax.all_to_all(
        flagged.reshape(req_count, page_cap, page_width + flag_cols),
        "req",
        split_axis=0,
        concat_axis=0,
        tiled=True,
    ).reshape(pool_count, page_width + flag_cols)
    incoming = arrived[:, :page_width]
    incoming_filled = arrived[:, page_width]
    slot_ids = slot_perm[0]
    placing = (slot_ids[None, :] == jnp.arange(pool_count, dtype=jnp.int32)[:, None]) & (
        incoming_filled[None, :] > 0
    )
    written = jnp.dot(
        placing.astype(jnp.bfloat16), incoming, preferred_element_type=jnp.float32
    ).astype(jnp.bfloat16)
    written_mask = jnp.any(placing, axis=1)
    pool_pages = cache_pool.reshape(pool_count, page_width)
    new_pool = jnp.where(written_mask[:, None], written, pool_pages).reshape(cache_pool.shape)
    local_keys = jnp.concatenate([key_value, prefix_cache], axis=0)
    blocks = [local_keys]
    for shift_by in range(1, SPAN + 1):
        blocks.append(from_behind(local_keys, "req", shift_by))
    key_segs = []
    key_poss = []
    for step_back in range(SPAN + 1):
        block_id = req_index - step_back
        seg_new, pos_new = label_rows(block_id * tok_rows + row_ids, starts, prefix_lengths)
        seg_old, pos_old = prefix_rows(block_id, tok_rows, prefix_count, starts, prefix_lengths)
        key_segs.extend([seg_new, seg_old])
        key_poss.extend([pos_new, pos_old])
    key_segment = jnp.concatenate(key_segs)
    key_position = jnp.concatenate(key_poss)
    allowed = (key_segment[None, :] == segment[:, None]) & (
        key_position[None, :] <= position[:, None]
    )
    allowed = allowed & (
        (position[:, None] - key_position[None, :] < WINDOW) | (key_position[None, :] < SINKS)
    )
    all_keys = jnp.concatenate(blocks, axis=0)
    attended = head_attention(queries, all_keys[:, 0, :], all_keys[:, 1, :], allowed)
    hidden = jax.nn.gelu(lifted + fc1_bias, approximate=True).astype(jnp.bfloat16)
    contract_rows = (((1,), (1,)), ((), ()))
    attn_part = lax.dot_general(
        attended, dense_full_t, contract_rows, preferred_element_type=jnp.float32
    )
    mlp_part = lax.dot_general(
        hidden, fc2_full_t, contract_rows, preferred_element_type=jnp.float32
    )
    branches = attn_part + mlp_part
    summed = lax.psum_scatter(branches, "tensor", scatter_dimension=1, tiled=True)
    layer_out = (tokens.astype(jnp.float32) + summed + dense_bias + fc2_bias).astype(jnp.bfloat16)
    return (layer_out, new_pool)


def solution(mesh):
    placed = (
        P("req", "tensor"),
        P("req"),
        P(),
        P("req", None),
        P("req", None),
        P(),
        P(),
        P("req", None, "tensor"),
        P(None, "tensor"),
        P("tensor", "req"),
        P("tensor"),
        P("req", "tensor"),
        P("tensor"),
        P("tensor", "req"),
        P("tensor"),
        P("req", None, "tensor"),
        P("req", None, "tensor"),
    )
    return jax.shard_map(
        shards,
        mesh=mesh,
        in_specs=placed,
        out_specs=(P("req", "tensor"), P("req", None, "tensor")),
        check_vma=False,
    )
```

profile of v0, /device:TPU:6, one launch (start us, length us, event | category | flops | bytes accessed | tf_op | source)
XLA Modules:
  0.0 319.7 jit_solution(9198134115274271958)
XLA Ops:
  13.4 1.1 copy.42
  14.5 30.4 %all-gather.3.cloned.1.call-done = bf16[256,2048]{1,0:T(8,128)(2,1)} async-done(((bf16[256,256]{1,0:T(8,128)(2,1)}), bf16[256,2048]{1,0:T(8,128)(2,1)}) %all-gather.3.cloned.1.call-update) | async-done | bytes 1048592 | tf_op jit(solution)/shard_map/all_gather | solution.py:118
  45.0 1.5 convert_reduce_fusion
  46.5 1.6 fusion.25
  48.1 160.8 %all-gather.5.cloned.1.call-done = bf16[2048,2176]{1,0:T(8,128)(2,1)} async-done(((bf16[32,2176]{1,0:T(8,128)(2,1)}), bf16[2048,2176]{1,0:T(8,128)(2,1)}) %all-gather.5.cloned.1.call-update) | async-done | bytes 8912912 | tf_op jit(solution)/shard_map/all_gather | solution.py:139
  209.0 3.0 fusion.32
  215.6 1.7 constant_dynamic-update-slice_fusion.14
  217.4 1.9 constant_dynamic-update-slice_fusion.8
  219.8 3.6 %collective-permute-start.1 = (bf16[512,2,256]{0,2,1:T(8,128)(2,1)S(1)}, bf16[512,2,256]{0,2,1:T(8,128)(2,1)S(1)}, u32[]{:S(2)}, u32[]{:S(2)}) collective-permute-start(bf16[512,2,256]{0,2,1:T(8,128)(2,1)S(1)} %pad_maximum_fusion.2), channel_id=1, source_target_pairs={{0,16},{8,24},{16,32},{24,40},{32,48},{40,56},{48,64},{56,72},{64,... | collective-permute-start | bytes 1572872 | tf_op jit(solution)/shard_map/ppermute | solution.py:18
  223.4 2.0 collective-permute-start
  225.5 1.8 constant_dynamic-update-slice_fusion.6
  227.4 5.3 %collective-permute-done.1 = bf16[512,2,256]{0,2,1:T(8,128)(2,1)S(1)} collective-permute-done((bf16[512,2,256]{0,2,1:T(8,128)(2,1)S(1)}, bf16[512,2,256]{0,2,1:T(8,128)(2,1)S(1)}, u32[]{:S(2)}, u32[]{:S(2)}) %collective-permute-start.1) | collective-permute-done | bytes 524320 | tf_op jit(solution)/shard_map/ppermute | solution.py:18
  232.7 5.6 %collective-permute-done = bf16[512,2,256]{0,2,1:T(8,128)(2,1)S(1)} collective-permute-done((bf16[512,2,256]{0,2,1:T(8,128)(2,1)S(1)}, bf16[512,2,256]{0,2,1:T(8,128)(2,1)S(1)}, u32[]{:S(2)}, u32[]{:S(2)}) %collective-permute-start) | collective-permute-done | bytes 524320 | tf_op jit(solution)/shard_map/ppermute | solution.py:18
  239.3 15.9 %while.11 = (s32[]{:T(128)}, bf16[4,256,64]{1,2,0:T(8,128)(2,1)S(1)}, s32[4]{0:T(128)S(1)}, bf16[256,256]{0,1:T(8,128)(2,1)S(1)}, bf16[1536,256]{0,1:T(8,128)(2,...) while((s32[]{:T(128)}, ...), condition=%wide.region_25.26_spmd.clone, body=%wide.region_22.25_spmd.clone.sunk | while | flops 112492032 | bytes 5240535 | solution.py:88
  241.5 0.9 fusion.96
  245.4 0.9 fusion.96
  249.4 0.9 fusion.96
  255.9 1.8 fusion.38
  257.7 5.1 %convolution_add_fusion = f32[256,2048]{1,0:T(8,128)} fusion(f32[256,2048]{1,0:T(8,128)S(1)} %fusion.38, bf16[2048,2176]{1,0:T(8,128)(2,1)} %all-gather.5.cloned.1.call-done, f32[512]{0:T(512)S(1)} %copy-done.13, bf16[256,2048]{1,0:T(8,128)(2,1)S(1)} %copy-done, f32[2048]{0:T(1024)S(1)} %copy-done.11, f32[2048]{0:T(1024)S(1)} %copy-done.12, ...), kind=kOutput, calls=%fused_computation.23 | convolution fusion | flops 1078722560 | bytes 9457664 | tf_op jit(solution)/shard_map/dot_general | solution.py:231
  264.9 1.0 reshape.258
  265.9 12.5 %all-to-all-start = ((bf16[64,2,2176]{2,1,0:T(2,128)(2,1)}), bf16[64,2,2176]{2,1,0:T(2,128)(2,1)S(1)}, u32[]{:S(2)}, u32[]{:S(2)}) async-start(bf16[64,2,2176]{2,1,0:T(2,128)(2,1)} %reshape.258), calls=%async_computation.1 | async-start | bytes 1114112 | tf_op jit(solution)/shard_map/all_to_all | solution.py:185
  278.9 30.7 %all-to-all-done = bf16[64,2,2176]{2,1,0:T(2,128)(2,1)S(1)} async-done(((bf16[64,2,2176]{2,1,0:T(2,128)(2,1)}), bf16[64,2,2176]{2,1,0:T(2,128)(2,1)S(1)}, u32[]{:S(2)}, u32[]{:S(2)}) %all-to-all-start) | async-done | bytes 557088 | tf_op jit(solution)/shard_map/all_to_all | solution.py:185
  310.3 1.2 reshape.261
  311.5 1.6 add_convert_fusion
  (116 shorter events, 25.4 us)
Async XLA Ops:
  7.2 201.8 %copy-start.11 = (f32[2048]{0:T(1024)S(1)}, f32[2048]{0:T(1024)}, u32[]{:S(2)}) copy-start(f32[2048]{0:T(1024)} %param.25) | copy-start | bytes 24580
  7.2 201.8 %copy-start.12 = (f32[2048]{0:T(1024)S(1)}, f32[2048]{0:T(1024)}, u32[]{:S(2)}) copy-start(f32[2048]{0:T(1024)} %param.24) | copy-start | bytes 24580
  7.2 37.8 %all-gather.3.cloned.1.call-start = ((), (), s32[]{:S(2)}) async-start(), calls=%async_computation.2 | async-start | bytes 1179648 | tf_op jit(solution)/shard_map/all_gather | solution.py:118
  7.9 201.0 %all-gather.5.cloned.1.call-start = ((), (), s32[]{:S(2)}) async-start(), calls=%async_computation.3 | async-start | bytes 9052160 | tf_op jit(solution)/shard_map/all_gather | solution.py:139
  11.9 0.7 copy-start.3
  12.6 298.9 %reduce-scatter.2.cloned.1.call-start = ((), (), s32[]{:S(2)}) async-start(), calls=%async_computation.4 | async-start | bytes 2359296 | tf_op jit(solution)/shard_map/reduce_scatter | solution.py:235
  45.0 164.0 %copy-start = (bf16[256,2048]{1,0:T(8,128)(2,1)S(1)}, bf16[256,2048]{1,0:T(8,128)(2,1)}, u32[]{:S(2)}) copy-start(bf16[256,2048]{1,0:T(8,128)(2,1)} %all-gather.3.cloned.1.call-done) | copy-start | bytes 3145732
  212.0 1.0 slice-start
  212.3 1.8 copy-start.7
  219.8 12.9 %collective-permute-start.1 = (bf16[512,2,256]{0,2,1:T(8,128)(2,1)S(1)}, bf16[512,2,256]{0,2,1:T(8,128)(2,1)S(1)}, u32[]{:S(2)}, u32[]{:S(2)}) collective-permute-start(bf16[512,2,256]{0,2,1:T(8,128)(2,1)S(1)} %pad_maximum_fusion.2), channel_id=1, source_target_pairs={{0,16},{8,24},{16,32},{24,40},{32,48},{40,56},{48,64},{56,72},{64,... | collective-permute-start | bytes 1572872 | tf_op jit(solution)/shard_map/ppermute | solution.py:18
  223.4 14.9 %collective-permute-start = (bf16[512,2,256]{0,2,1:T(8,128)(2,1)S(1)}, bf16[512,2,256]{0,2,1:T(8,128)(2,1)S(1)}, u32[]{:S(2)}, u32[]{:S(2)}) collective-permute-start(bf16[512,2,256]{0,2,1:T(8,128)(2,1)S(1)} %pad_maximum_fusion.2), channel_id=1, source_target_pairs={{0,8},{8,16},{16,24},{24,32},{32,40},{40,48},{48,56},{56,64},{64,7... | collective-permute-start | bytes 1572872 | tf_op jit(solution)/shard_map/ppermute | solution.py:18
  238.4 0.9 copy-start.4
  255.2 0.7 copy-start.5
  255.2 2.4 copy-start.13
  262.8 0.7 copy-start.6
  264.3 14.1 %copy-start.1 = (bf16[512,2,256]{2,1,0:T(2,128)(2,1)S(1)}, bf16[512,2,256]{2,1,0:T(2,128)(2,1)}, u32[]{:S(2)}) copy-start(bf16[512,2,256]{2,1,0:T(2,128)(2,1)} %param.35) | copy-start | bytes 1572868
  264.9 45.0 %copy-start.10 = (s32[1,128]{1,0:T(1,128)S(1)}, s32[1,128]{1,0:T(1,128)}, u32[]{:S(2)}) copy-start(s32[1,128]{1,0:T(1,128)} %param.23) | copy-start | bytes 1540
  265.9 43.7 %all-to-all-start = ((bf16[64,2,2176]{2,1,0:T(2,128)(2,1)}), bf16[64,2,2176]{2,1,0:T(2,128)(2,1)S(1)}, u32[]{:S(2)}, u32[]{:S(2)}) async-start(bf16[64,2,2176]{2,1,0:T(2,128)(2,1)} %reshape.258), calls=%async_computation.1 | async-start | bytes 1114112 | tf_op jit(solution)/shard_map/all_to_all | solution.py:185
  278.8 32.7 %copy-start.2 = (bf16[256,256]{1,0:T(8,128)(2,1)S(1)}, bf16[256,256]{1,0:T(8,128)(2,1)}, u32[]{:S(2)}) copy-start(bf16[256,256]{1,0:T(8,128)(2,1)} %param.19) | copy-start | bytes 393220
  278.8 32.7 %copy-start.8 = (f32[256]{0:T(256)S(1)}, f32[256]{0:T(256)}, u32[]{:S(2)}) copy-start(f32[256]{0:T(256)} %param.33) | copy-start | bytes 3076
  278.9 32.7 %copy-start.9 = (f32[256]{0:T(256)S(1)}, f32[256]{0:T(256)}, u32[]{:S(2)}) copy-start(f32[256]{0:T(256)} %param.29) | copy-start | bytes 3076
Sparse Core Ops, SparseCore 0:
  10.1 34.7 all-gather.2
  48.5 160.4 all-gather.4
  262.9 36.6 reduce-scatter.1
where the time goes:
time: 321 us; the launch traced here: 320 us
  waiting for transfers between devices  234 us (73%)
  other arithmetic  18.5 us (6%)
  starting transfers between devices  18.3 us (6%)
  matrix products  17.8 us (6%)
  local copies, waits for them, and re-layouts  14.5 us (5%)
  between operations  14.3 us (4%)
    all_gather x1, waiting for transfers between devices, shards(): everything = lax.all_gather(packed, 'req', axis=0, tiled=True)  161 us
    all_to_all x1, waiting for transfers between devices, shards(): lax.all_to_all(flagged.reshape(req_count, page_cap, page_width + flag_col...  30.7 us
    all_gather x1, waiting for transfers between devices, shards(): gathered = lax.all_gather(tokens, 'tensor', axis=1, tiled=True)  30.4 us
    all_to_all x1, starting transfers between devices, shards(): lax.all_to_all(flagged.reshape(req_count, page_cap, page_width + flag_col...  12.5 us
    ppermute x2, waiting for transfers between devices, from_behind(): lax.ppermute(value, axis, [(source, source + steps) for source in range(l...  10.9 us
  transfers between devices with their start and end apart: 6, of which 5 were waited for; matrix products, arithmetic and copies ran while one was open for 5% of the time, Pallas kernels for 0%

commit v1 on v0

--- a/solution.py
+++ b/solution.py
@@ -115,7 +115,23 @@
     head_cols = qkv_weight.shape[2]
     pool_count = slot_perm.shape[1]
     page_cap = pool_count // req_count
-    gathered = lax.all_gather(tokens, "tensor", axis=1, tiled=True)
+    ways, here, turn = (lax.axis_size("tensor"), lax.axis_index("tensor"), tokens.shape[1])
+    shape = [n * ways if d == 1 else n for d, n in enumerate(tokens.shape)]
+    full = lax.dynamic_update_slice_in_dim(
+        jnp.zeros(shape, tokens.dtype), tokens, here * turn, axis=1
+    )
+    going_up = going_down = tokens
+    for far in range(1, ways // 2 + 1):
+        going_up = lax.ppermute(going_up, "tensor", [(d, (d + 1) % ways) for d in range(ways)])
+        full = lax.dynamic_update_slice_in_dim(full, going_up, (here - far) % ways * turn, axis=1)
+        if 2 * far < ways:
+            going_down = lax.ppermute(
+                going_down, "tensor", [(d, (d - 1) % ways) for d in range(ways)]
+            )
+            full = lax.dynamic_update_slice_in_dim(
+                full, going_down, (here + far) % ways * turn, axis=1
+            )
+    gathered = full
     normed = norm_rows(gathered.astype(jnp.float32), ln_gain, ln_bias)
     row_ids = jnp.arange(tok_rows, dtype=jnp.int32)
     places = req_index * tok_rows + row_ids

time: 321 us -> 288 us (0.90)
  waiting for transfers between devices: 234 us -> 185 us
  starting transfers between devices: 18.3 us -> 32.8 us
    all_gather x1 -> x0, waiting for transfers between devices: 30.4 us -> none  [shards(): gathered = lax.all_gather(tokens, 'tensor', axis=1, tiled=True)]
    all_gather x1, waiting for transfers between devices: 161 us -> 141 us  [shards(): everything = lax.all_gather(packed, 'req', axis=0, tiled=True)]
    ppermute x0 -> x7, starting transfers between devices: none -> 14.5 us  [the longest x4 12.8 us: shards(): lax.ppermute(going_up, 'tensor', [(d, (d + 1) % ways) for d in range(ways)])]
    unnamed x35 -> x61, local copies, waits for them, and re-layouts: 6.12 us -> 6.68 us
  transfers between devices with their start and end apart: 6 -> 12, of which waited for: 5 -> 7; matrix products, arithmetic and copies ran while one was open for 5% -> 4% of each run, Pallas kernels for 0% -> 0%
where the time goes in v1:
time: 288 us; the launch traced here: 287 us
  waiting for transfers between devices  185 us (64%)
  starting transfers between devices  32.8 us (11%)
  other arithmetic  18.5 us (6%)
  matrix products  17.8 us (6%)
  local copies, waits for them, and re-layouts  15.3 us (5%)
  between operations  14.8 us (5%)
    all_gather x1, waiting for transfers between devices, shards(): everything = lax.all_gather(packed, 'req', axis=0, tiled=True)  141 us
    all_to_all x1, waiting for transfers between devices, shards(): lax.all_to_all(flagged.reshape(req_count, page_cap, page_width + flag_col...  30.7 us
    ppermute x4, starting transfers between devices, shards(): lax.ppermute(going_up, 'tensor', [(d, (d + 1) % ways) for d in range(ways)])  12.8 us
    all_to_all x1, starting transfers between devices, shards(): lax.all_to_all(flagged.reshape(req_count, page_cap, page_width + flag_col...  12.6 us
    ppermute x2, waiting for transfers between devices, from_behind(): lax.ppermute(value, axis, [(source, source + steps) for source in range(l...  10.2 us
    unnamed x61, local copies, waits for them, and re-layouts  6.68 us
  transfers between devices with their start and end apart: 12, of which 7 were waited for; matrix products, arithmetic and copies ran while one was open for 4% of the time, Pallas kernels for 0%

profile of v1, /device:TPU:6, one launch (start us, length us, event | category | flops | bytes accessed | tf_op | source)
XLA Modules:
  0.0 287.0 jit_solution(4324024249835949497)
XLA Ops:
  12.0 1.7 collective-permute-start.1
  16.1 1.1 copy.42
  17.4 4.2 %collective-permute-start.2 = (bf16[256,256]{1,0:T(8,128)(2,1)S(1)}, bf16[256,256]{1,0:T(8,128)(2,1)S(1)}, u32[]{:S(2)}, u32[]{:S(2)}) collective-permute-start(bf16[256,256]{1,0:T(8,128)(2,1)S(1)} %collective-permute-done), channel_id=1, source_target_pairs={{0,1},{1,2},{2,3},{3,4},{4,5},{5,6},{6,7},{7,0},{8,9},{9,10},{10,1... | collective-permute-start | bytes 393224 | tf_op jit(solution)/shard_map/ppermute | solution.py:125
  21.7 0.9 collective-permute-done.2
  22.7 3.9 %collective-permute-start.4 = (bf16[256,256]{1,0:T(8,128)(2,1)S(1)}, bf16[256,256]{1,0:T(8,128)(2,1)S(1)}, u32[]{:S(2)}, u32[]{:S(2)}) collective-permute-start(bf16[256,256]{1,0:T(8,128)(2,1)S(1)} %collective-permute-done.2), channel_id=1, source_target_pairs={{0,1},{1,2},{2,3},{3,4},{4,5},{5,6},{6,7},{7,0},{8,9},{9,10},{10,1... | collective-permute-start | bytes 393224 | tf_op jit(solution)/shard_map/ppermute | solution.py:125
  26.6 0.9 collective-permute-done.4
  27.6 4.6 %collective-permute-start.6 = (bf16[256,256]{1,0:T(8,128)(2,1)S(1)}, bf16[256,256]{1,0:T(8,128)(2,1)S(1)}, u32[]{:S(2)}, u32[]{:S(2)}) collective-permute-start(bf16[256,256]{1,0:T(8,128)(2,1)S(1)} %collective-permute-done.4), channel_id=1, source_target_pairs={{0,1},{1,2},{2,3},{3,4},{4,5},{5,6},{6,7},{7,0},{8,9},{9,10},{10,1... | collective-permute-start | bytes 393224 | tf_op jit(solution)/shard_map/ppermute | solution.py:125
  33.9 141.4 %all-gather.2.cloned.1.call-done = bf16[2048,2176]{1,0:T(8,128)(2,1)} async-done(((bf16[32,2176]{1,0:T(8,128)(2,1)}), bf16[2048,2176]{1,0:T(8,128)(2,1)}) %all-gather.2.cloned.1.call-update) | async-done | bytes 8912912 | tf_op jit(solution)/shard_map/all_gather | solution.py:155
  175.2 3.0 %fusion.32 = f32[256,768]{1,0:T(8,128)S(1)} fusion(bf16[2048,2176]{1,0:T(8,128)(2,1)} %all-gather.2.cloned.1.call-done, f32[768]{0:T(1024)S(1)} %add.274, bf16[256,2048]{1,0:T(8,128)(2,1)S(1)} %constant_dynamic-update-slice_fusion.16, f32[2048]{0:T(1024)S(1)} %copy-done.24, f32[2048]{0:T(1024)S(1)} %copy-done.26, f32[256]{0:T(256)S(1)} %add_rsqrt_fusion, ...), kind=kOutput, calls=%fused_computation.39 | convolution fusion | flops 808648704 | bytes 5002240 | tf_op jit(solution)/shard_map/dot_general | solution.py:167
  181.9 1.7 constant_dynamic-update-slice_fusion.14
  183.7 2.0 constant_dynamic-update-slice_fusion.8
  186.7 3.6 %collective-permute-start.8 = (bf16[512,2,256]{0,2,1:T(8,128)(2,1)S(1)}, bf16[512,2,256]{0,2,1:T(8,128)(2,1)S(1)}, u32[]{:S(2)}, u32[]{:S(2)}) collective-permute-start(bf16[512,2,256]{0,2,1:T(8,128)(2,1)S(1)} %pad_maximum_fusion.2), channel_id=1, source_target_pairs={{0,16},{8,24},{16,32},{24,40},{32,48},{40,56},{48,64},{56,72},{64,... | collective-permute-start | bytes 1572872 | tf_op jit(solution)/shard_map/ppermute | solution.py:18
  190.4 2.0 collective-permute-start.7
  192.5 1.7 constant_dynamic-update-slice_fusion.6
  195.1 4.5 %collective-permute-done.8 = bf16[512,2,256]{0,2,1:T(8,128)(2,1)S(1)} collective-permute-done((bf16[512,2,256]{0,2,1:T(8,128)(2,1)S(1)}, bf16[512,2,256]{0,2,1:T(8,128)(2,1)S(1)}, u32[]{:S(2)}, u32[]{:S(2)}) %collective-permute-start.8) | collective-permute-done | bytes 524320 | tf_op jit(solution)/shard_map/ppermute | solution.py:18
  199.7 5.6 %collective-permute-done.7 = bf16[512,2,256]{0,2,1:T(8,128)(2,1)S(1)} collective-permute-done((bf16[512,2,256]{0,2,1:T(8,128)(2,1)S(1)}, bf16[512,2,256]{0,2,1:T(8,128)(2,1)S(1)}, u32[]{:S(2)}, u32[]{:S(2)}) %collective-permute-start.7) | collective-permute-done | bytes 524320 | tf_op jit(solution)/shard_map/ppermute | solution.py:18
  206.3 15.9 %while.11 = (s32[]{:T(128)}, bf16[4,256,64]{1,2,0:T(8,128)(2,1)S(1)}, s32[4]{0:T(128)S(1)}, bf16[256,256]{0,1:T(8,128)(2,1)S(1)}, bf16[1536,256]{0,1:T(8,128)(2,...) while((s32[]{:T(128)}, ...), condition=%wide.region_25.26_spmd.clone, body=%wide.region_22.25_spmd.clone.sunk | while | flops 112492032 | bytes 5240535 | solution.py:88
  222.8 1.8 fusion.38
  224.6 5.1 %convolution_add_fusion = f32[256,2048]{1,0:T(8,128)} fusion(f32[256,2048]{1,0:T(8,128)S(1)} %fusion.38, bf16[2048,2176]{1,0:T(8,128)(2,1)} %all-gather.2.cloned.1.call-done, f32[512]{0:T(512)} %param.31, bf16[256,2048]{1,0:T(8,128)(2,1)S(1)} %constant_dynamic-update-slice_fusion.16, f32[2048]{0:T(1024)S(1)} %copy-done.25, f32[2048]{0:T(1024)} %param.24, ...), kind=kOutput, calls=%fused_computation.23 | convolution fusion | flops 1078722560 | bytes 9457664 | tf_op jit(solution)/shard_map/dot_general | solution.py:247
  231.9 1.0 reshape.258
  232.9 12.6 %all-to-all-start = ((bf16[64,2,2176]{2,1,0:T(2,128)(2,1)}), bf16[64,2,2176]{2,1,0:T(2,128)(2,1)S(1)}, u32[]{:S(2)}, u32[]{:S(2)}) async-start(bf16[64,2,2176]{2,1,0:T(2,128)(2,1)} %reshape.258), calls=%async_computation.1 | async-start | bytes 1114112 | tf_op jit(solution)/shard_map/all_to_all | solution.py:201
  245.9 30.7 %all-to-all-done = bf16[64,2,2176]{2,1,0:T(2,128)(2,1)S(1)} async-done(((bf16[64,2,2176]{2,1,0:T(2,128)(2,1)}), bf16[64,2,2176]{2,1,0:T(2,128)(2,1)S(1)}, u32[]{:S(2)}, u32[]{:S(2)}) %all-to-all-start) | async-done | bytes 557088 | tf_op jit(solution)/shard_map/all_to_all | solution.py:201
  277.3 1.2 reshape.261
  278.5 1.6 add_convert_fusion
  (162 shorter events, 32.3 us)
Async XLA Ops:
  7.2 10.2 %copy-start.1 = (bf16[256,256]{1,0:T(8,128)(2,1)S(1)}, bf16[256,256]{1,0:T(8,128)(2,1)}, u32[]{:S(2)}) copy-start(bf16[256,256]{1,0:T(8,128)(2,1)} %param.19) | copy-start | bytes 393220
  7.2 168.0 %all-gather.2.cloned.1.call-start = ((), (), s32[]{:S(2)}) async-start(), calls=%async_computation.2 | async-start | bytes 9052160 | tf_op jit(solution)/shard_map/all_gather | solution.py:155
  8.1 3.8 %copy-start.11 = (s32[256]{0:T(256)}, s32[256]{0:T(256)S(1)}, u32[]{:S(2)}) copy-start(s32[256]{0:T(256)S(1)} %iota_add_fusion.2) | copy-start | bytes 3076
  11.9 266.6 %reduce-scatter.2.cloned.1.call-start = ((), (), s32[]{:S(2)}) async-start(), calls=%async_computation.3 | async-start | bytes 2359296 | tf_op jit(solution)/shard_map/reduce_scatter | solution.py:251
  12.0 5.5 %collective-permute-start = (bf16[256,256]{1,0:T(8,128)(2,1)}, bf16[256,256]{1,0:T(8,128)(2,1)S(1)}, u32[]{:S(2)}, u32[]{:S(2)}) collective-permute-start(bf16[256,256]{1,0:T(8,128)(2,1)} %param.19), channel_id=1, source_target_pairs={{0,1},{1,2},{2,3},{3,4},{4,5},{5,6},{6,7},{7,0},{8,9},{9,10},{10,1... | collective-permute-start | bytes 393224 | tf_op jit(solution)/shard_map/ppermute | solution.py:125
  12.0 9.7 %collective-permute-start.1 = (bf16[256,256]{1,0:T(8,128)(2,1)}, bf16[256,256]{1,0:T(8,128)(2,1)S(1)}, u32[]{:S(2)}, u32[]{:S(2)}) collective-permute-start(bf16[256,256]{1,0:T(8,128)(2,1)} %param.19), channel_id=1, source_target_pairs={{0,7},{1,0},{2,1},{3,2},{4,3},{5,4},{6,5},{7,6},{8,15},{9,8},{10,9... | collective-permute-start | bytes 393224 | tf_op jit(solution)/shard_map/ppermute | solution.py:128
  17.4 157.9 %copy-start.24 = (f32[2048]{0:T(1024)S(1)}, f32[2048]{0:T(1024)}, u32[]{:S(2)}) copy-start(f32[2048]{0:T(1024)} %param.25) | copy-start | bytes 24580
  17.4 157.8 %copy-start.26 = (f32[2048]{0:T(1024)S(1)}, f32[2048]{0:T(1024)}, u32[]{:S(2)}) copy-start(f32[2048]{0:T(1024)} %param.24) | copy-start | bytes 24580
  17.4 5.2 %collective-permute-start.2 = (bf16[256,256]{1,0:T(8,128)(2,1)S(1)}, bf16[256,256]{1,0:T(8,128)(2,1)S(1)}, u32[]{:S(2)}, u32[]{:S(2)}) collective-permute-start(bf16[256,256]{1,0:T(8,128)(2,1)S(1)} %collective-permute-done), channel_id=1, source_target_pairs={{0,1},{1,2},{2,3},{3,4},{4,5},{5,6},{6,7},{7,0},{8,9},{9,10},{10,1... | collective-permute-start | bytes 393224 | tf_op jit(solution)/shard_map/ppermute | solution.py:125
  21.7 4.9 %collective-permute-start.3 = (bf16[256,256]{1,0:T(8,128)(2,1)S(1)}, bf16[256,256]{1,0:T(8,128)(2,1)S(1)}, u32[]{:S(2)}, u32[]{:S(2)}) collective-permute-start(bf16[256,256]{1,0:T(8,128)(2,1)S(1)} %collective-permute-done.1), channel_id=1, source_target_pairs={{0,7},{1,0},{2,1},{3,2},{4,3},{5,4},{6,5},{7,6},{8,15},{9,8},{10,9... | collective-permute-start | bytes 393224 | tf_op jit(solution)/shard_map/ppermute | solution.py:128
  22.7 4.9 %collective-permute-start.4 = (bf16[256,256]{1,0:T(8,128)(2,1)S(1)}, bf16[256,256]{1,0:T(8,128)(2,1)S(1)}, u32[]{:S(2)}, u32[]{:S(2)}) collective-permute-start(bf16[256,256]{1,0:T(8,128)(2,1)S(1)} %collective-permute-done.2), channel_id=1, source_target_pairs={{0,1},{1,2},{2,3},{3,4},{4,5},{5,6},{6,7},{7,0},{8,9},{9,10},{10,1... | collective-permute-start | bytes 393224 | tf_op jit(solution)/shard_map/ppermute | solution.py:125
  26.6 5.6 %collective-permute-start.5 = (bf16[256,256]{1,0:T(8,128)(2,1)S(1)}, bf16[256,256]{1,0:T(8,128)(2,1)S(1)}, u32[]{:S(2)}, u32[]{:S(2)}) collective-permute-start(bf16[256,256]{1,0:T(8,128)(2,1)S(1)} %collective-permute-done.3), channel_id=1, source_target_pairs={{0,7},{1,0},{2,1},{3,2},{4,3},{5,4},{6,5},{7,6},{8,15},{9,8},{10,9... | collective-permute-start | bytes 393224 | tf_op jit(solution)/shard_map/ppermute | solution.py:128
  27.6 5.6 %collective-permute-start.6 = (bf16[256,256]{1,0:T(8,128)(2,1)S(1)}, bf16[256,256]{1,0:T(8,128)(2,1)S(1)}, u32[]{:S(2)}, u32[]{:S(2)}) collective-permute-start(bf16[256,256]{1,0:T(8,128)(2,1)S(1)} %collective-permute-done.4), channel_id=1, source_target_pairs={{0,1},{1,2},{2,3},{3,4},{4,5},{5,6},{6,7},{7,0},{8,9},{9,10},{10,1... | collective-permute-start | bytes 393224 | tf_op jit(solution)/shard_map/ppermute | solution.py:125
  33.4 141.8 %copy-start.13 = (f32[256]{0:T(256)}, f32[256]{0:T(256)S(1)}, u32[]{:S(2)}) copy-start(f32[256]{0:T(256)S(1)} %broadcast_multiply_fusion) | copy-start | bytes 3076
  33.8 141.4 %copy-start.19 = (f32[256]{0:T(256)}, f32[256]{0:T(256)S(1)}, u32[]{:S(2)}) copy-start(f32[256]{0:T(256)S(1)} %add_rsqrt_fusion) | copy-start | bytes 3076
  178.6 7.9 %copy-start.22 = (f32[16]{0:T(128)S(1)}, f32[16]{0:T(128)}, u32[]{:S(2)}) copy-start(f32[16]{0:T(128)} %multiply_power_fusion) | copy-start | bytes 196
  181.9 4.0 %copy-start.5 = (s32[256]{0:T(256)}, s32[256]{0:T(256)S(1)}, u32[]{:S(2)}) copy-start(s32[256]{0:T(256)S(1)} %get-tuple-element.255) | copy-start | bytes 3076
  186.7 12.9 %collective-permute-start.8 = (bf16[512,2,256]{0,2,1:T(8,128)(2,1)S(1)}, bf16[512,2,256]{0,2,1:T(8,128)(2,1)S(1)}, u32[]{:S(2)}, u32[]{:S(2)}) collective-permute-start(bf16[512,2,256]{0,2,1:T(8,128)(2,1)S(1)} %pad_maximum_fusion.2), channel_id=1, source_target_pairs={{0,16},{8,24},{16,32},{24,40},{32,48},{40,56},{48,64},{56,72},{64,... | collective-permute-start | bytes 1572872 | tf_op jit(solution)/shard_map/ppermute | solution.py:18
  190.4 14.9 %collective-permute-start.7 = (bf16[512,2,256]{0,2,1:T(8,128)(2,1)S(1)}, bf16[512,2,256]{0,2,1:T(8,128)(2,1)S(1)}, u32[]{:S(2)}, u32[]{:S(2)}) collective-permute-start(bf16[512,2,256]{0,2,1:T(8,128)(2,1)S(1)} %pad_maximum_fusion.2), channel_id=1, source_target_pairs={{0,8},{8,16},{16,24},{24,32},{32,40},{40,48},{48,56},{56,64},{64,7... | collective-permute-start | bytes 1572872 | tf_op jit(solution)/shard_map/ppermute | solution.py:18
  231.3 14.2 %copy-start = (bf16[512,2,256]{2,1,0:T(2,128)(2,1)S(1)}, bf16[512,2,256]{2,1,0:T(2,128)(2,1)}, u32[]{:S(2)}) copy-start(bf16[512,2,256]{2,1,0:T(2,128)(2,1)} %param.35) | copy-start | bytes 1572868
  231.9 45.0 %copy-start.21 = (s32[1,128]{1,0:T(1,128)S(1)}, s32[1,128]{1,0:T(1,128)}, u32[]{:S(2)}) copy-start(s32[1,128]{1,0:T(1,128)} %param.23) | copy-start | bytes 1540
  232.9 43.7 %all-to-all-start = ((bf16[64,2,2176]{2,1,0:T(2,128)(2,1)}), bf16[64,2,2176]{2,1,0:T(2,128)(2,1)S(1)}, u32[]{:S(2)}, u32[]{:S(2)}) async-start(bf16[64,2,2176]{2,1,0:T(2,128)(2,1)} %reshape.258), calls=%async_computation.1 | async-start | bytes 1114112 | tf_op jit(solution)/shard_map/all_to_all | solution.py:201
  245.9 32.7 %copy-start.17 = (f32[256]{0:T(256)S(1)}, f32[256]{0:T(256)}, u32[]{:S(2)}) copy-start(f32[256]{0:T(256)} %param.33) | copy-start | bytes 3076
  245.9 32.6 %copy-start.18 = (f32[256]{0:T(256)S(1)}, f32[256]{0:T(256)}, u32[]{:S(2)}) copy-start(f32[256]{0:T(256)} %param.29) | copy-start | bytes 3076
  (16 other events, 28.2 us)
Sparse Core Ops, SparseCore 0:
  12.0 163.1 all-gather.1
  229.9 36.6 reduce-scatter.1
